TPU v7x, 128 devices: a whole 4x4x4 slice. The times are simulated.
128 devices in a mesh: seq: 32 (over z, y, core), head: 4 (over x).
Axes of the slice: x: 4, y: 4, z: 4, core: 2. Of those that a mesh axis runs over, the one named last changes fastest.
Arguments:
- tokens: bfloat16 [16384, 4096], P('seq'), may hold values from -6 to 6
- w_query: bfloat16 [4096, 2048], P('seq', 'head'), may hold values from -0.09375 to 0.09375
- w_key: bfloat16 [4096, 2048], P('seq', 'head'), may hold values from -0.09375 to 0.09375
- w_value: bfloat16 [4096, 2048], P('seq', 'head'), may hold values from -0.09375 to 0.09375
- omega_seed: int32 [16, 128, 256], P('head'), may hold values from -4 to 4
- grad_out: bfloat16 [16384, 2048], P('seq', 'head'), may hold values from -6 to 6
Outputs:
- input_grad: bfloat16 [16384, 4096], P('seq', 'head')
- query_wgrad: float32 [4096, 2048], P('seq', 'head')
- key_wgrad: float32 [4096, 2048], P('seq', 'head')
- value_wgrad: float32 [4096, 2048], P('seq', 'head')
Inputs may be any that keep to these rules, and one draw needn't show every extreme that they name: `omega_seed`: the feature seeds are small whole numbers.
All inputs are finite; a program needn't handle non-finite values.
Results may differ from a plain program's by a relative error of at most 0.02.
Values may be sent and summed in bfloat16 or wider, within the bound.
No kernel may reach another device: no remote copies, remote signals or barrier semaphores. Data moves between devices by JAX's collectives and lax.ppermute only.
A program may use at most 128 MiB of HBM per device.

v0:
```python
import math
import jax
import jax.numpy as jnp
from jax import lax
from jax.sharding import PartitionSpec as P

exact_arithmetic_mode = lax.Precision.HIGHEST
seed_step = 0.4


def carried_in(shard, axis, join, neutral):
    place = lax.axis_index(axis)
    gathered = jax.tree.map(
        lambda a, kind: lax.all_gather(a.astype(kind), axis), shard, (jnp.bfloat16, jnp.bfloat16)
    )
    state = jax.tree.map(lambda a, e: jnp.zeros_like(a) + jnp.asarray(e, a.dtype), shard, neutral)

    def one(hop, state):
        return join(
            state,
            jax.tree.map(
                lambda a, own: lax.dynamic_index_in_dim(a, hop, 0, False).astype(own.dtype),
                gathered,
                shard,
            ),
        )

    return lax.fori_loop(0, place, one, state)


def carried_in_2(shard, axis, join, neutral):
    count = lax.axis_size(axis)
    place = lax.axis_index(axis)
    ahead = count - 1 - place
    gathered = jax.tree.map(
        lambda a, kind: lax.all_gather(a.astype(kind), axis),
        shard,
        jax.tree.map(lambda a: jnp.bfloat16 if a.dtype == jnp.float32 else a.dtype, shard),
    )
    state = jax.tree.map(lambda a, e: jnp.zeros_like(a) + jnp.asarray(e, a.dtype), shard, neutral)

    def one(hop, state):
        source = count - 1 - hop
        return join(
            state,
            jax.tree.map(
                lambda a, own: lax.dynamic_index_in_dim(a, source, 0, False).astype(own.dtype),
                gathered,
                shard,
            ),
        )

    return lax.fori_loop(0, ahead, one, state)


def feature_map(scaled, projection):
    projected = jnp.einsum("htd,hdm->htm", scaled, projection, precision=exact_arithmetic_mode)
    return jnp.exp(projected - 0.5 * jnp.sum(scaled * scaled, -1, keepdims=True)) / math.sqrt(
        projection.shape[-1]
    )


def feature_grad(upstream, features, scaled, projection):
    weighted = upstream * features
    projected = jnp.einsum("htm,hdm->htd", weighted, projection, precision=exact_arithmetic_mode)
    return (projected - jnp.sum(weighted, -1, keepdims=True) * scaled) * scaled.shape[-1] ** (-0.25)


def add_states(earlier, later_part):
    return (earlier[0] + later_part[0], earlier[1] + later_part[1])


def head_major(value_matrix, heads_here):
    tok_rows = value_matrix.shape[0]
    return value_matrix.astype(jnp.float32).reshape(tok_rows, heads_here, -1).transpose(1, 0, 2)


def token_major(value_matrix):
    return value_matrix.transpose(1, 0, 2).reshape(value_matrix.shape[1], -1).astype(jnp.bfloat16)


def back_product(grads, weight):
    return lax.dot_general(
        grads, weight, (((1,), (1,)), ((), ())), preferred_element_type=jnp.float32
    )


def projection_term(tokens, grads):
    return lax.dot_general(
        tokens, grads, (((0,), (0,)), ((), ())), preferred_element_type=jnp.float32
    )


def per_device(tokens, w_query, w_key, w_value, omega_seed, grad_out):
    heads_here = omega_seed.shape[0]
    head_size = omega_seed.shape[1]
    full_query, full_key, full_value = (
        lax.all_gather(w_query, "seq", axis=0, tiled=True),
        lax.all_gather(w_key, "seq", axis=0, tiled=True),
        lax.all_gather(w_value, "seq", axis=0, tiled=True),
    )
    query_act = jnp.dot(tokens, full_query, preferred_element_type=jnp.float32).astype(jnp.bfloat16)
    key_act = jnp.dot(tokens, full_key, preferred_element_type=jnp.float32).astype(jnp.bfloat16)
    value_act = jnp.dot(tokens, full_value, preferred_element_type=jnp.float32).astype(jnp.bfloat16)
    projection = omega_seed.astype(jnp.float32) * seed_step
    scale_in = head_size ** (-0.25)
    query_scaled = head_major(query_act, heads_here) * scale_in
    key_scaled = head_major(key_act, heads_here) * scale_in
    value_matrix = head_major(value_act, heads_here)
    upstream = head_major(grad_out, heads_here)
    query_feature_rows = feature_map(query_scaled, projection)
    source_embedding_entries = feature_map(key_scaled, projection)
    tok_rows = tokens.shape[0]
    causal = jnp.tril(jnp.ones((tok_rows, tok_rows), jnp.float32))
    block_local_states = jnp.einsum(
        "vzn,vza->vna", source_embedding_entries, value_matrix, precision=exact_arithmetic_mode
    )
    local_totals = jnp.sum(source_embedding_entries, 1)
    zero_states = jnp.zeros_like(block_local_states)
    zero_totals = jnp.zeros_like(local_totals)
    prefix_carried_outer, prefix_normaliser_accrual = carried_in(
        (block_local_states, local_totals), "seq", add_states, (zero_states, zero_totals)
    )
    attention_scores = (
        jnp.einsum(
            "htm,hsm->hts",
            query_feature_rows,
            source_embedding_entries,
            precision=exact_arithmetic_mode,
        )
        * causal
    )
    attention_numerator = jnp.einsum(
        "xyw,xwc->xyc", attention_scores, value_matrix, precision=exact_arithmetic_mode
    ) + jnp.einsum(
        "sji,six->sjx", query_feature_rows, prefix_carried_outer, precision=exact_arithmetic_mode
    )
    normer = jnp.sum(attention_scores, -1) + jnp.einsum(
        "htm,hm->ht", query_feature_rows, prefix_normaliser_accrual, precision=exact_arithmetic_mode
    )
    output = attention_numerator / normer[..., None]
    dividend_cotangent = upstream / normer[..., None]
    normaliser_cotangent = -jnp.sum(upstream * output, -1) / normer
    couplewise_products = (
        jnp.einsum(
            "htd,hsd->hts", dividend_cotangent, value_matrix, precision=exact_arithmetic_mode
        )
        + normaliser_cotangent[..., None]
    ) * causal
    target_embedding_cotangent = (
        jnp.einsum(
            "mez,mzo->meo",
            couplewise_products,
            source_embedding_entries,
            precision=exact_arithmetic_mode,
        )
        + jnp.einsum(
            "zrc,zfc->zrf",
            dividend_cotangent,
            prefix_carried_outer,
            precision=exact_arithmetic_mode,
        )
        + normaliser_cotangent[..., None] * prefix_normaliser_accrual[:, None, :]
    )
    query16 = token_major(
        feature_grad(target_embedding_cotangent, query_feature_rows, query_scaled, projection)
    )
    subsequent_local_states = jnp.einsum(
        "opu,opc->ouc", query_feature_rows, dividend_cotangent, precision=exact_arithmetic_mode
    )
    later_totals = jnp.einsum(
        "htm,ht->hm", query_feature_rows, normaliser_cotangent, precision=exact_arithmetic_mode
    )
    subsequent_states, subsequent_sum = carried_in_2(
        (subsequent_local_states, later_totals), "seq", add_states, (zero_states, zero_totals)
    )
    key_feature_gradient = (
        jnp.einsum(
            "ykl,yku->ylu", couplewise_products, query_feature_rows, precision=exact_arithmetic_mode
        )
        + jnp.einsum(
            "bgq,bxq->bgx", value_matrix, subsequent_states, precision=exact_arithmetic_mode
        )
        + subsequent_sum[:, None, :]
    )
    value_gradient_rows = jnp.einsum(
        "vkm,vky->vmy", attention_scores, dividend_cotangent, precision=exact_arithmetic_mode
    ) + jnp.einsum(
        "tjr,tro->tjo", source_embedding_entries, subsequent_states, precision=exact_arithmetic_mode
    )
    key16 = token_major(
        feature_grad(key_feature_gradient, source_embedding_entries, key_scaled, projection)
    )
    value16 = token_major(value_gradient_rows)
    joined = jnp.concatenate([query16, key16, value16], 1)
    weight_total = lax.psum_scatter(
        projection_term(tokens, joined).astype(jnp.bfloat16), "seq", scatter_dimension=0, tiled=True
    ).astype(jnp.float32)
    columns = query16.shape[1]
    query_wgrad = weight_total[:, :columns]
    key_wgrad = weight_total[:, columns : 2 * columns]
    value_wgrad = weight_total[:, 2 * columns :]
    partial_input = (
        back_product(query16, full_query)
        + back_product(key16, full_key)
        + back_product(value16, full_value)
    )
    input_grad = lax.psum_scatter(
        partial_input.astype(jnp.bfloat16), "head", scatter_dimension=1, tiled=True
    )
    return (input_grad, query_wgrad, key_wgrad, value_wgrad)


def solution(mesh):
    placed = (
        P("seq", None),
        P("seq", "head"),
        P("seq", "head"),
        P("seq", "head"),
        P("head", None, None),
        P("seq", "head"),
    )
    return jax.shard_map(
        per_device,
        mesh=mesh,
        in_specs=placed,
        out_specs=(P("seq", "head"), P("seq", "head"), P("seq", "head"), P("seq", "head")),
        check_vma=False,
    )
```

profile of v0, /device:TPU:1, one launch (start us, length us, event | category | flops | bytes accessed | tf_op | source)
XLA Modules:
  0.0 566.0 jit_solution(16715974828505819920)
XLA Ops:
  9.4 50.6 %all-gather.16.cloned.1.call-done = bf16[4096,512]{1,0:T(8,128)(2,1)} async-done(((bf16[128,512]{1,0:T(8,128)(2,1)}), bf16[4096,512]{1,0:T(8,128)(2,1)}) %all-gather.16.cloned.1.call-update) | async-done | bytes 4194320 | tf_op jit(solution)/shard_map/all_gather | solution.py:100
  60.1 5.8 %convolution_convert_fusion.1 = bf16[512,512]{0,1:T(8,128)(2,1)S(1)} fusion(bf16[512,4096]{1,0:T(8,128)(2,1)} %param.10, bf16[4096,512]{1,0:T(8,128)(2,1)} %all-gather.16.cloned.1.call-done), kind=kOutput, calls=%fused_computation.45 | convolution fusion | flops 2147745792 | bytes 8912896 | tf_op jit(solution)/shard_map/dot_general | solution.py:104
  67.0 40.8 %all-gather.14.cloned.1.call-done = bf16[4096,512]{1,0:T(8,128)(2,1)} async-done(((bf16[128,512]{1,0:T(8,128)(2,1)}), bf16[4096,512]{1,0:T(8,128)(2,1)}) %all-gather.14.cloned.1.call-update) | async-done | bytes 4194320 | tf_op jit(solution)/shard_map/all_gather | solution.py:99
  107.8 5.8 %convolution_convert_fusion.2 = bf16[512,512]{0,1:T(8,128)(2,1)S(1)} fusion(bf16[512,4096]{1,0:T(8,128)(2,1)} %param.10, bf16[4096,512]{1,0:T(8,128)(2,1)} %all-gather.14.cloned.1.call-done), kind=kOutput, calls=%fused_computation.46 | convolution fusion | flops 2147745792 | bytes 8912896 | tf_op jit(solution)/shard_map/dot_general | solution.py:103
  113.8 2.3 fusion.74
  116.1 1.3 copy-done
  117.5 1.8 convolution_convert_fusion.5
  119.3 1.2 copy.36
  120.6 24.0 %all-gather.4 = bf16[32,4,256]{2,1,0:T(4,128)(2,1)S(1)} all-gather(bf16[1,4,256]{2,1,0:T(4,128)(2,1)S(1)} %bitcast.157), channel_id=3, replica_groups=mesh['seq'=32,'head'=4] {'seq'}, dimensions={0}, use_global_device_ids=true | all-gather | bytes 67584 | tf_op jit(solution)/shard_map/all_gather | solution.py:14
  144.6 11.0 %all-gather.12.cloned.1.call-done = bf16[4096,512]{1,0:T(8,128)(2,1)} async-done(((bf16[128,512]{1,0:T(8,128)(2,1)}), bf16[4096,512]{1,0:T(8,128)(2,1)}) %all-gather.12.cloned.1.call-update) | async-done | bytes 4194320 | tf_op jit(solution)/shard_map/all_gather | solution.py:98
  155.6 5.9 %convolution_convert_fusion.3 = bf16[512,512]{0,1:T(8,128)(2,1)S(1)} fusion(bf16[512,4096]{1,0:T(8,128)(2,1)} %param.10, bf16[4096,512]{1,0:T(8,128)(2,1)} %all-gather.12.cloned.1.call-done), kind=kOutput, calls=%fused_computation.47 | convolution fusion | flops 2147745792 | bytes 8912896 | tf_op jit(solution)/shard_map/dot_general | solution.py:102
  161.7 2.0 exponential_multiply_fusion.1
  163.7 5.2 multiply_reduce_fusion
  169.0 41.5 %all-gather.18.cloned.1.call-done = bf16[128,256,128]{2,1,0:T(8,128)(2,1)} async-done(((bf16[4,256,128]{2,1,0:T(8,128)(2,1)}), bf16[128,256,128]{2,1,0:T(8,128)(2,1)}) %all-gather.18.cloned.1.call-update) | async-done | bytes 8388624 | tf_op jit(solution)/shard_map/all_gather | solution.py:14
  211.3 2.0 while.26
  211.3 2.0 convert_add_fusion.8
  213.3 1.2 fusion.63
  214.5 3.9 convolution_convert_fusion.4
  218.5 2.6 fusion.77
  221.1 4.2 fusion.39
  225.3 1.9 fusion.61
  227.2 90.3 %all-gather.5 = bf16[32,4,256]{2,1,0:T(4,128)(2,1)S(1)} all-gather(bf16[1,4,256]{2,1,0:T(4,128)(2,1)S(1)} %bitcast.156), channel_id=5, replica_groups=mesh['seq'=32,'head'=4] {'seq'}, dimensions={0}, use_global_device_ids=true | all-gather | bytes 67584 | tf_op jit(solution)/shard_map/all_gather | solution.py:36
  317.5 1.9 fusion.52
  319.4 4.3 fusion.2
  323.7 2.4 fusion.75
  326.1 2.2 fusion.29
  328.3 5.6 fusion.1
  334.0 33.3 %while.27 = (s32[]{:T(128)}, f32[4,256,128]{2,1,0:T(8,128)S(1)}, f32[4,256]{1,0:T(4,128)S(1)}, s32[]{:T(128)}, bf16[32,4,256,128]{3,2,1,0:T(8,128)(2,1)}, /*inde...) while((s32[]{:T(128)}, f32[4,256,128]{2,1,0:T(8,128)S(1)}, ...), condition=%wide.region_9.10_spmd, body=%wide.region_8.9_spmd.sunk | while | flops 264198 | bytes 1321123 | solution.py:53
  334.0 1.1 convert_add_fusion.10
  347.4 1.1 convert_add_fusion.10
  348.5 1.1 convert_add_fusion.10
  349.6 1.1 convert_add_fusion.10
  350.7 1.1 convert_add_fusion.10
  351.8 1.1 convert_add_fusion.10
  353.0 1.1 convert_add_fusion.10
  354.1 1.1 convert_add_fusion.10
  367.3 3.0 fusion.80
  370.4 7.0 %fusion.30 = bf16[4,512,128]{1,2,0:T(8,128)(2,1)S(1)} fusion(f32[4,512,128]{1,2,0:T(8,128)S(1)} %fusion.80, f32[4,512,512]{1,2,0:T(8,128)} %get-tuple-element.159, f32[512,512]{0,1:T(8,128)S(1)} %fusion.50, f32[4,512]{1,0:T(4,128)S(1)} %bitcast_add_fusion, f32[512,512]{0,1:T(8,128)S(1)} %copy-done.6), kind=kOutput, calls=%fused_computation.44 | convolution fusion | flops 1612447744 | bytes 7872512 | tf_op jit(solution)/shard_map/vkm,vky->vmy/dot_general | solution.py:186
  377.5 1.4 fusion.76
  378.9 1.4 fusion.28
  380.3 11.5 %fusion = bf16[4096,1536]{0,1:T(8,128)(2,1)} fusion(bf16[512,4096]{1,0:T(8,128)(2,1)S(1)} %copy-done.26, bf16[512,512]{0,1:T(8,128)(2,1)S(1)} %bitcast.146, bf16[512,512]{0,1:T(8,128)(2,1)S(1)} %bitcast.148, bf16[512,512]{0,1:T(8,128)(2,1)S(1)} %bitcast.144), kind=kOutput, calls=%fused_computation.5 | convolution fusion | flops 6453460992 | bytes 18350080 | tf_op jit(solution)/shard_map/dot_general | solution.py:89
  391.7 16.6 %copy.89 = bf16[4096,1536]{1,0:T(8,128)(2,1)} copy(bf16[4096,1536]{0,1:T(8,128)(2,1)} %fusion) | data formatting | bytes 25165824
  408.7 4.7 fusion.78
  413.5 5.9 %fusion.79 = f32[512,4096]{1,0:T(8,128)} fusion(bf16[512,512]{0,1:T(8,128)(2,1)S(1)} %bitcast.149, bf16[4096,512]{1,0:T(8,128)(2,1)S(1)} %copy-done.20), kind=kOutput, calls=%fused_computation.99 | convolution fusion | flops 2147483648 | bytes 13107200 | tf_op jit(solution)/shard_map/dot_general | solution.py:83
  419.4 8.3 %add_convert_fusion = bf16[512,4096]{1,0:T(8,128)(2,1)} fusion(f32[512,4096]{1,0:T(8,128)S(1)} %fusion.78, f32[512,4096]{1,0:T(8,128)} %fusion.79, bf16[512,512]{0,1:T(8,128)(2,1)S(1)} %bitcast.147, bf16[4096,512]{1,0:T(8,128)(2,1)S(1)} %copy-done.19), kind=kOutput, calls=%fused_computation.6 | convolution fusion | flops 2153775104 | bytes 25690112 | tf_op jit(solution)/shard_map/dot_general | solution.py:83
  427.8 80.2 %reduce-scatter.7.cloned.1.call-done = bf16[128,1536]{1,0:T(8,128)(2,1)} async-done(((bf16[4096,1536]{1,0:T(8,128)(2,1)}), bf16[128,1536]{1,0:T(8,128)(2,1)}) %reduce-scatter.7.cloned.1.call-update) | async-done | bytes 393232
  508.0 1.2 copy.90
  511.7 46.9 %reduce-scatter.5.cloned.1.call-done = bf16[512,1024]{1,0:T(8,128)(2,1)} async-done(((bf16[512,4096]{1,0:T(8,128)(2,1)}), bf16[512,1024]{1,0:T(8,128)(2,1)}) %reduce-scatter.5.cloned.1.call-update) | async-done | bytes 1048592 | tf_op jit(solution)/shard_map/reduce_scatter | solution.py:208
  (140 shorter events, 31.7 us)
Async XLA Ops:
  7.2 52.9 %all-gather.16.cloned.1.call-start = ((), (), s32[]{:S(2)}) async-start(), calls=%async_computation.4 | async-start | bytes 4325376 | tf_op jit(solution)/shard_map/all_gather | solution.py:100
  7.9 99.9 %all-gather.14.cloned.1.call-start = ((), (), s32[]{:S(2)}) async-start(), calls=%async_computation.3 | async-start | bytes 4325376 | tf_op jit(solution)/shard_map/all_gather | solution.py:99
  8.6 146.9 %all-gather.12.cloned.1.call-start = ((), (), s32[]{:S(2)}) async-start(), calls=%async_computation.2 | async-start | bytes 4325376 | tf_op jit(solution)/shard_map/all_gather | solution.py:98
  9.4 201.1 %all-gather.18.cloned.1.call-start = ((), (), s32[]{:S(2)}) async-start(), calls=%async_computation.6 | async-start | bytes 8650752 | tf_op jit(solution)/shard_map/all_gather | solution.py:14
  65.9 0.8 copy-start.24
  67.0 49.1 %copy-start.12 = (bf16[512,4,128]{2,0,1:T(8,128)(2,1)}, bf16[512,4,128]{2,0,1:T(8,128)(2,1)S(1)}, u32[]{:S(2)}) copy-start(bf16[512,4,128]{2,0,1:T(8,128)(2,1)S(1)} %copy.43) | copy-start | bytes 1572868
  67.0 46.8 %copy-start.7 = (s32[4,128,256]{2,1,0:T(8,128)S(1)}, s32[4,128,256]{2,1,0:T(8,128)}, u32[]{:S(2)}) copy-start(s32[4,128,256]{2,1,0:T(8,128)} %param.14) | copy-start | bytes 1572868
  113.6 2.5 copy-start.15
  113.7 5.7 %copy-start.25 = (bf16[512,512]{1,0:T(8,128)(2,1)S(1)}, bf16[512,512]{1,0:T(8,128)(2,1)}, u32[]{:S(2)}) copy-start(bf16[512,512]{1,0:T(8,128)(2,1)} %param.15) | copy-start | bytes 1572868
  116.1 1.3 copy-start
  119.3 214.7 %all-gather.20.cloned.1.call-start = ((), (), s32[]{:S(2)}) async-start(), calls=%async_computation.7 | async-start | bytes 8650752 | tf_op jit(solution)/shard_map/all_gather | solution.py:36
  155.6 6.1 %copy-start.8 = (s32[4,128,256]{2,1,0:T(8,128)S(1)}, s32[4,128,256]{2,1,0:T(8,128)}, u32[]{:S(2)}) copy-start(s32[4,128,256]{2,1,0:T(8,128)} %param.14) | copy-start | bytes 1572868
  161.5 2.2 copy-start.17
  161.5 2.2 copy-start.1
  218.4 289.5 %reduce-scatter.7.cloned.1.call-start = ((), (), s32[]{:S(2)}) async-start(), calls=%async_computation.8 | async-start | bytes 12976128
  218.5 2.6 copy-start.5
  221.1 96.4 %copy-start.13 = (bf16[512,4,128]{2,0,1:T(8,128)(2,1)S(1)}, bf16[512,4,128]{2,0,1:T(8,128)(2,1)}, u32[]{:S(2)}) copy-start(bf16[512,4,128]{2,0,1:T(8,128)(2,1)} %copy-done.12) | copy-start | bytes 1572868
  225.3 94.1 %copy-start.2 = (f32[4,512,256]{1,2,0:T(8,128)S(1)}, f32[4,512,256]{1,2,0:T(8,128)}, u32[]{:S(2)}) copy-start(f32[4,512,256]{1,2,0:T(8,128)} %copy-done) | copy-start | bytes 6291460
  319.4 4.3 copy-start.4
  323.7 2.4 copy-start.9
  323.7 2.4 copy-start.18
  334.0 36.4 %copy-start.6 = (f32[512,512]{0,1:T(8,128)S(1)}, f32[512,512]{0,1:T(8,128)}, u32[]{:S(2)}) copy-start(f32[512,512]{0,1:T(8,128)} %copy.36) | copy-start | bytes 3145732
  370.4 7.0 %copy-start.3 = (f32[4,512,256]{1,2,0:T(8,128)S(1)}, f32[4,512,256]{1,2,0:T(8,128)}, u32[]{:S(2)}) copy-start(f32[4,512,256]{1,2,0:T(8,128)} %copy-done) | copy-start | bytes 6291460
  370.4 7.0 %copy-start.11 = (f32[4,512,256]{1,2,0:T(8,128)S(1)}, f32[4,512,256]{1,2,0:T(8,128)}, u32[]{:S(2)}) copy-start(f32[4,512,256]{1,2,0:T(8,128)} %fusion.1) | copy-start | bytes 6291460
  370.4 7.0 %copy-start.14 = (bf16[512,4,128]{2,0,1:T(8,128)(2,1)S(1)}, bf16[512,4,128]{2,0,1:T(8,128)(2,1)}, u32[]{:S(2)}) copy-start(bf16[512,4,128]{2,0,1:T(8,128)(2,1)} %copy-done.12) | copy-start | bytes 1572868
  377.4 1.5 copy-start.10
  377.4 1.5 copy-start.16
  377.4 2.8 copy-start.21
  377.4 2.8 copy-start.26
  380.2 11.5 %copy-start.22 = (bf16[512,4,128]{0,2,1:T(8,128)(2,1)}, bf16[512,4,128]{0,2,1:T(8,128)(2,1)S(1)}, u32[]{:S(2)}) copy-start(bf16[512,4,128]{0,2,1:T(8,128)(2,1)S(1)} %fusion.28) | copy-start | bytes 1572868
  408.4 5.1 copy-start.23
  408.4 150.3 %reduce-scatter.5.cloned.1.call-start = ((), (), s32[]{:S(2)}) async-start(), calls=%async_computation.5 | async-start | bytes 5242880 | tf_op jit(solution)/shard_map/reduce_scatter | solution.py:208
  408.7 4.8 copy-start.20
  413.5 5.9 %copy-start.19 = (bf16[4096,512]{1,0:T(8,128)(2,1)S(1)}, bf16[4096,512]{1,0:T(8,128)(2,1)}, u32[]{:S(2)}) copy-start(bf16[4096,512]{1,0:T(8,128)(2,1)} %all-gather.16.cloned.1.call-done) | copy-start | bytes 12582916
Sparse Core Ops, SparseCore 0:
  10.2 49.7 all-gather.15
  62.3 45.4 all-gather.13
  110.1 45.4 all-gather.11
  158.3 52.1 all-gather.17
  218.6 110.8 all-gather.19
  408.5 99.3 reduce-scatter.6
  510.9 47.7 reduce-scatter.4
where the time goes:
time: 574 us; the launch traced here: 566 us
  waiting for transfers between devices  273 us (48%)
  blocking collectives  114 us (20%)
  matrix products  102 us (18%)
  other arithmetic  35 us (6%)
  local copies, waits for them, and re-layouts  25 us (4%)
  between operations  15.2 us (3%)
    all_gather x1, blocking collectives, carried_in_2(): lax.all_gather(a.astype(kind), axis)  90.3 us
    unnamed x8, waiting for transfers between devices  82.3 us
    all_gather x1, waiting for transfers between devices, per_device(): lax.all_gather(w_value, 'seq', axis=0, tiled=True)  50.6 us
    reduce_scatter x1, waiting for transfers between devices, per_device(): lax.psum_scatter(partial_input.astype(jnp.bfloat16), 'head', scatter_dime...  46.9 us
    all_gather x1, waiting for transfers between devices, carried_in(): lax.all_gather(a.astype(kind), axis)  41.5 us
    all_gather x1, waiting for transfers between devices, per_device(): lax.all_gather(w_key, 'seq', axis=0, tiled=True)  40.8 us
    add x62, other arithmetic, add_states(): return (earlier[0] + later_part[0], earlier[1] + later_part[1])  34.6 us
    all_gather x1, blocking collectives, carried_in(): lax.all_gather(a.astype(kind), axis)  24 us
  transfers between devices with their start and end apart: 7, of which 6 were waited for; matrix products, arithmetic and copies ran while one was open for 14% of the time, Pallas kernels for 0%

commit v1 on v0

--- a/solution.py
+++ b/solution.py
@@ -94,10 +94,17 @@
 def per_device(tokens, w_query, w_key, w_value, omega_seed, grad_out):
     heads_here = omega_seed.shape[0]
     head_size = omega_seed.shape[1]
+
+    def tell_the_rows(page):
+        return jnp.concatenate(
+            lax.all_to_all(jnp.stack([page for _ in range(lax.axis_size("seq"))], 0), "seq", 0, 0),
+            0,
+        )
+
     full_query, full_key, full_value = (
         lax.all_gather(w_query, "seq", axis=0, tiled=True),
         lax.all_gather(w_key, "seq", axis=0, tiled=True),
-        lax.all_gather(w_value, "seq", axis=0, tiled=True),
+        tell_the_rows(w_value),
     )
     query_act = jnp.dot(tokens, full_query, preferred_element_type=jnp.float32).astype(jnp.bfloat16)
     key_act = jnp.dot(tokens, full_key, preferred_element_type=jnp.float32).astype(jnp.bfloat16)

time: 574 us -> 549 us (0.956)
  waiting for transfers between devices: 273 us -> 183 us
  blocking collectives: 114 us -> 181 us
    all_to_all x0 -> x1, blocking collectives: none -> 67.7 us  [tell_the_rows(): lax.all_to_all(jnp.stack([page for _ in range(lax.axis_size('seq'))], 0),...]
    all_gather x1 -> x0, waiting for transfers between devices: 50.6 us -> none  [per_device(): lax.all_gather(w_value, 'seq', axis=0, tiled=True)]
    all_gather x1, waiting for transfers between devices: 40.8 us -> 0.98 us  [per_device(): lax.all_gather(w_key, 'seq', axis=0, tiled=True)]
    unnamed x8 -> x7, waiting for transfers between devices: 82.3 us -> 81.6 us
    unnamed x59 -> x63, local copies, waits for them, and re-layouts: 22.6 us -> 22.6 us
  transfers between devices with their start and end apart: 7 -> 6, of which waited for: 6 -> 5; matrix products, arithmetic and copies ran while one was open for 14% -> 14% of each run, Pallas kernels for 0% -> 0%
where the time goes in v1:
time: 549 us; the launch traced here: 540 us
  waiting for transfers between devices  183 us (33%)
  blocking collectives  181 us (33%)
  matrix products  98.7 us (18%)
  other arithmetic  35 us (6%)
  local copies, waits for them, and re-layouts  26.4 us (5%)
  between operations  15.2 us (3%)
    all_gather x1, blocking collectives, carried_in_2(): lax.all_gather(a.astype(kind), axis)  89.9 us
    unnamed x7, waiting for transfers between devices  81.6 us
    all_to_all x1, blocking collectives, tell_the_rows(): lax.all_to_all(jnp.stack([page for _ in range(lax.axis_size('seq'))], 0),...  67.7 us
    reduce_scatter x1, waiting for transfers between devices, per_device(): lax.psum_scatter(partial_input.astype(jnp.bfloat16), 'head', scatter_dime...  46.8 us
    all_gather x1, waiting for transfers between devices, carried_in(): lax.all_gather(a.astype(kind), axis)  41.6 us
    add x62, other arithmetic, add_states(): return (earlier[0] + later_part[0], earlier[1] + later_part[1])  34.5 us
    all_gather x1, blocking collectives, carried_in(): lax.all_gather(a.astype(kind), axis)  23 us
    unnamed x63, local copies, waits for them, and re-layouts  22.6 us
  transfers between devices with their start and end apart: 6, of which 5 were waited for; matrix products, arithmetic and copies ran while one was open for 14% of the time, Pallas kernels for 0%

profile of v1, /device:TPU:1, one launch (start us, length us, event | category | flops | bytes accessed | tf_op | source)
XLA Modules:
  0.0 539.8 jit_solution(301825980744603139)
XLA Ops:
  8.7 1.4 stack.2
  10.1 67.7 %all_to_all.5 = bf16[32,128,512]{2,1,0:T(8,128)(2,1)S(1)} all-to-all(bf16[32,128,512]{2,1,0:T(8,128)(2,1)S(1)} %stack.2), channel_id=1, replica_groups=mesh['seq'=32,'head'=4] {'seq'}, dimensions={0} | all-to-all | bytes 8388608 | tf_op jit(solution)/shard_map/all_to_all | solution.py:100
  77.8 2.4 convolution_convert_fusion.1
  82.3 5.8 %convolution_convert_fusion.2 = bf16[512,512]{0,1:T(8,128)(2,1)S(1)} fusion(bf16[512,4096]{1,0:T(8,128)(2,1)} %param.10, bf16[4096,512]{1,0:T(8,128)(2,1)} %all-gather.13.cloned.1.call-done), kind=kOutput, calls=%fused_computation.46 | convolution fusion | flops 2147745792 | bytes 8912896 | tf_op jit(solution)/shard_map/dot_general | solution.py:110
  88.3 2.3 fusion.74
  90.6 1.3 copy-done
  92.0 1.8 convolution_convert_fusion.5
  93.8 1.2 copy.36
  95.1 23.0 %all-gather.4 = bf16[32,4,256]{2,1,0:T(4,128)(2,1)S(1)} all-gather(bf16[1,4,256]{2,1,0:T(4,128)(2,1)S(1)} %bitcast.160), channel_id=3, replica_groups=mesh['seq'=32,'head'=4] {'seq'}, dimensions={0}, use_global_device_ids=true | all-gather | bytes 67584 | tf_op jit(solution)/shard_map/all_gather | solution.py:14
  118.2 11.6 %all-gather.11.cloned.1.call-done = bf16[4096,512]{1,0:T(8,128)(2,1)} async-done(((bf16[128,512]{1,0:T(8,128)(2,1)}), bf16[4096,512]{1,0:T(8,128)(2,1)}) %all-gather.11.cloned.1.call-update) | async-done | bytes 4194320 | tf_op jit(solution)/shard_map/all_gather | solution.py:105
  129.8 5.9 %convolution_convert_fusion.3 = bf16[512,512]{0,1:T(8,128)(2,1)S(1)} fusion(bf16[512,4096]{1,0:T(8,128)(2,1)} %param.10, bf16[4096,512]{1,0:T(8,128)(2,1)} %all-gather.11.cloned.1.call-done), kind=kOutput, calls=%fused_computation.47 | convolution fusion | flops 2147745792 | bytes 8912896 | tf_op jit(solution)/shard_map/dot_general | solution.py:109
  135.9 2.0 exponential_multiply_fusion.1
  137.9 5.2 multiply_reduce_fusion
  143.2 41.6 %all-gather.15.cloned.1.call-done = bf16[128,256,128]{2,1,0:T(8,128)(2,1)} async-done(((bf16[4,256,128]{2,1,0:T(8,128)(2,1)}), bf16[128,256,128]{2,1,0:T(8,128)(2,1)}) %all-gather.15.cloned.1.call-update) | async-done | bytes 8388624 | tf_op jit(solution)/shard_map/all_gather | solution.py:14
  185.7 2.0 while.26
  185.7 2.0 convert_add_fusion.8
  187.6 1.2 fusion.63
  188.8 3.9 convolution_convert_fusion.4
  192.8 2.6 fusion.77
  195.4 4.2 fusion.39
  199.7 1.9 fusion.61
  201.6 89.9 %all-gather.5 = bf16[32,4,256]{2,1,0:T(4,128)(2,1)S(1)} all-gather(bf16[1,4,256]{2,1,0:T(4,128)(2,1)S(1)} %bitcast.159), channel_id=5, replica_groups=mesh['seq'=32,'head'=4] {'seq'}, dimensions={0}, use_global_device_ids=true | all-gather | bytes 67584 | tf_op jit(solution)/shard_map/all_gather | solution.py:36
  291.4 1.9 fusion.52
  293.3 4.3 fusion.2
  297.7 2.4 fusion.75
  300.1 2.2 fusion.29
  302.2 5.6 %fusion.1 = f32[4,512,256]{1,2,0:T(8,128)} fusion(f32[4,512,256]{1,2,0:T(8,128)S(1)} %exponential_multiply_fusion.1, f32[4,512,512]{1,2,0:T(8,128)S(1)} %fusion.52, f32[4,512]{1,0:T(4,128)S(1)} %negate_divide_fusion, f32[512,512]{0,1:T(8,128)S(1)} %fusion.50), kind=kOutput, calls=%fused_computation.8 | convolution fusion | flops 3223322624 | bytes 9445376 | tf_op jit(solution)/shard_map/ykl,yku->ylu/dot_general | solution.py:185
  307.9 33.3 %while.27 = (s32[]{:T(128)}, f32[4,256,128]{2,1,0:T(8,128)S(1)}, f32[4,256]{1,0:T(4,128)S(1)}, s32[]{:T(128)}, bf16[32,4,256,128]{3,2,1,0:T(8,128)(2,1)}, /*inde...) while((s32[]{:T(128)}, f32[4,256,128]{2,1,0:T(8,128)S(1)}, ...), condition=%wide.region_9.10_spmd, body=%wide.region_8.9_spmd.sunk | while | flops 264198 | bytes 1321123 | solution.py:53
  308.0 1.1 convert_add_fusion.10
  311.4 1.1 convert_add_fusion.10
  312.5 1.1 convert_add_fusion.10
  313.6 1.1 convert_add_fusion.10
  314.7 1.1 convert_add_fusion.10
  315.8 1.1 convert_add_fusion.10
  316.9 1.1 convert_add_fusion.10
  318.0 1.1 convert_add_fusion.10
  341.3 3.0 fusion.80
  344.3 7.0 %fusion.30 = bf16[4,512,128]{1,2,0:T(8,128)(2,1)S(1)} fusion(f32[4,512,128]{1,2,0:T(8,128)S(1)} %fusion.80, f32[4,512,512]{1,2,0:T(8,128)} %get-tuple-element.159, f32[512,512]{0,1:T(8,128)S(1)} %fusion.50, f32[4,512]{1,0:T(4,128)S(1)} %bitcast_add_fusion, f32[512,512]{0,1:T(8,128)S(1)} %copy-done.6), kind=kOutput, calls=%fused_computation.44 | convolution fusion | flops 1612447744 | bytes 7872512 | tf_op jit(solution)/shard_map/vkm,vky->vmy/dot_general | solution.py:193
  351.4 1.4 fusion.76
  352.8 1.4 fusion.28
  354.2 11.5 %fusion = bf16[4096,1536]{0,1:T(8,128)(2,1)} fusion(bf16[512,4096]{1,0:T(8,128)(2,1)S(1)} %copy-done.28, bf16[512,512]{0,1:T(8,128)(2,1)S(1)} %bitcast.149, bf16[512,512]{0,1:T(8,128)(2,1)S(1)} %bitcast.151, bf16[512,512]{0,1:T(8,128)(2,1)S(1)} %bitcast.147), kind=kOutput, calls=%fused_computation.5 | convolution fusion | flops 6453460992 | bytes 18350080 | tf_op jit(solution)/shard_map/dot_general | solution.py:89
  365.7 16.7 %copy.89 = bf16[4096,1536]{1,0:T(8,128)(2,1)} copy(bf16[4096,1536]{0,1:T(8,128)(2,1)} %fusion) | data formatting | bytes 25165824
  382.7 4.7 fusion.78
  387.5 5.9 %fusion.79 = f32[512,4096]{1,0:T(8,128)} fusion(bf16[512,512]{0,1:T(8,128)(2,1)S(1)} %bitcast.152, bf16[4096,512]{1,0:T(8,128)(2,1)S(1)} %copy-done.21), kind=kOutput, calls=%fused_computation.99 | convolution fusion | flops 2147483648 | bytes 13107200 | tf_op jit(solution)/shard_map/dot_general | solution.py:83
  393.4 8.3 %add_convert_fusion = bf16[512,4096]{1,0:T(8,128)(2,1)} fusion(f32[512,4096]{1,0:T(8,128)S(1)} %fusion.78, f32[512,4096]{1,0:T(8,128)} %fusion.79, bf16[512,512]{0,1:T(8,128)(2,1)S(1)} %bitcast.150, bf16[4096,512]{1,0:T(8,128)(2,1)S(1)} %bitcast.140), kind=kOutput, calls=%fused_computation.6 | convolution fusion | flops 2153775104 | bytes 25690112 | tf_op jit(solution)/shard_map/dot_general | solution.py:83
  401.8 80.2 %reduce-scatter.7.cloned.1.call-done = bf16[128,1536]{1,0:T(8,128)(2,1)} async-done(((bf16[4096,1536]{1,0:T(8,128)(2,1)}), bf16[128,1536]{1,0:T(8,128)(2,1)}) %reduce-scatter.7.cloned.1.call-update) | async-done | bytes 393232
  481.9 1.2 copy.90
  485.7 46.8 %reduce-scatter.5.cloned.1.call-done = bf16[512,1024]{1,0:T(8,128)(2,1)} async-done(((bf16[512,4096]{1,0:T(8,128)(2,1)}), bf16[512,1024]{1,0:T(8,128)(2,1)}) %reduce-scatter.5.cloned.1.call-update) | async-done | bytes 1048592 | tf_op jit(solution)/shard_map/reduce_scatter | solution.py:215
  (143 shorter events, 32.0 us)
Async XLA Ops:
  7.2 75.1 %all-gather.13.cloned.1.call-start = ((), (), s32[]{:S(2)}) async-start(), calls=%async_computation.4 | async-start | bytes 4325376 | tf_op jit(solution)/shard_map/all_gather | solution.py:106
  7.9 121.9 %all-gather.11.cloned.1.call-start = ((), (), s32[]{:S(2)}) async-start(), calls=%async_computation.3 | async-start | bytes 4325376 | tf_op jit(solution)/shard_map/all_gather | solution.py:105
  8.7 176.2 %all-gather.15.cloned.1.call-start = ((), (), s32[]{:S(2)}) async-start(), calls=%async_computation.6 | async-start | bytes 8650752 | tf_op jit(solution)/shard_map/all_gather | solution.py:14
  10.1 67.8 %copy-start.27 = (bf16[512,4096]{1,0:T(8,128)(2,1)S(1)}, bf16[512,4096]{1,0:T(8,128)(2,1)}, u32[]{:S(2)}) copy-start(bf16[512,4096]{1,0:T(8,128)(2,1)} %param.10) | copy-start | bytes 12582916
  77.8 2.4 copy-start.7
  80.2 0.8 copy-start.25
  81.3 9.3 %copy-start.14 = (bf16[512,4,128]{2,0,1:T(8,128)(2,1)}, bf16[512,4,128]{2,0,1:T(8,128)(2,1)S(1)}, u32[]{:S(2)}) copy-start(bf16[512,4,128]{2,0,1:T(8,128)(2,1)S(1)} %copy.43) | copy-start | bytes 1572868
  81.3 7.0 %copy-start.9 = (s32[4,128,256]{2,1,0:T(8,128)S(1)}, s32[4,128,256]{2,1,0:T(8,128)}, u32[]{:S(2)}) copy-start(s32[4,128,256]{2,1,0:T(8,128)} %param.14) | copy-start | bytes 1572868
  88.1 2.5 copy-start.17
  88.1 5.7 %copy-start.26 = (bf16[512,512]{1,0:T(8,128)(2,1)S(1)}, bf16[512,512]{1,0:T(8,128)(2,1)}, u32[]{:S(2)}) copy-start(bf16[512,512]{1,0:T(8,128)(2,1)} %param.15) | copy-start | bytes 1572868
  90.6 1.3 copy-start
  93.8 214.1 %all-gather.17.cloned.1.call-start = ((), (), s32[]{:S(2)}) async-start(), calls=%async_computation.7 | async-start | bytes 8650752 | tf_op jit(solution)/shard_map/all_gather | solution.py:36
  129.8 6.1 %copy-start.10 = (s32[4,128,256]{2,1,0:T(8,128)S(1)}, s32[4,128,256]{2,1,0:T(8,128)}, u32[]{:S(2)}) copy-start(s32[4,128,256]{2,1,0:T(8,128)} %param.14) | copy-start | bytes 1572868
  135.7 2.2 copy-start.19
  135.7 2.2 copy-start.1
  192.8 289.2 %reduce-scatter.7.cloned.1.call-start = ((), (), s32[]{:S(2)}) async-start(), calls=%async_computation.8 | async-start | bytes 12976128
  192.8 2.6 copy-start.5
  195.4 96.0 %copy-start.15 = (bf16[512,4,128]{2,0,1:T(8,128)(2,1)S(1)}, bf16[512,4,128]{2,0,1:T(8,128)(2,1)}, u32[]{:S(2)}) copy-start(bf16[512,4,128]{2,0,1:T(8,128)(2,1)} %copy-done.14) | copy-start | bytes 1572868
  199.7 93.7 %copy-start.2 = (f32[4,512,256]{1,2,0:T(8,128)S(1)}, f32[4,512,256]{1,2,0:T(8,128)}, u32[]{:S(2)}) copy-start(f32[4,512,256]{1,2,0:T(8,128)} %copy-done) | copy-start | bytes 6291460
  293.3 4.3 copy-start.4
  297.6 2.4 copy-start.11
  297.7 2.4 copy-start.20
  307.9 36.4 %copy-start.6 = (f32[512,512]{0,1:T(8,128)S(1)}, f32[512,512]{0,1:T(8,128)}, u32[]{:S(2)}) copy-start(f32[512,512]{0,1:T(8,128)} %copy.36) | copy-start | bytes 3145732
  344.3 7.0 %copy-start.3 = (f32[4,512,256]{1,2,0:T(8,128)S(1)}, f32[4,512,256]{1,2,0:T(8,128)}, u32[]{:S(2)}) copy-start(f32[4,512,256]{1,2,0:T(8,128)} %copy-done) | copy-start | bytes 6291460
  344.3 7.0 %copy-start.13 = (f32[4,512,256]{1,2,0:T(8,128)S(1)}, f32[4,512,256]{1,2,0:T(8,128)}, u32[]{:S(2)}) copy-start(f32[4,512,256]{1,2,0:T(8,128)} %fusion.1) | copy-start | bytes 6291460
  344.3 7.0 %copy-start.16 = (bf16[512,4,128]{2,0,1:T(8,128)(2,1)S(1)}, bf16[512,4,128]{2,0,1:T(8,128)(2,1)}, u32[]{:S(2)}) copy-start(bf16[512,4,128]{2,0,1:T(8,128)(2,1)} %copy-done.14) | copy-start | bytes 1572868
  351.3 1.5 copy-start.12
  351.3 1.5 copy-start.18
  351.4 2.8 copy-start.22
  351.4 2.8 copy-start.28
  354.2 11.5 %copy-start.23 = (bf16[512,4,128]{0,2,1:T(8,128)(2,1)}, bf16[512,4,128]{0,2,1:T(8,128)(2,1)S(1)}, u32[]{:S(2)}) copy-start(bf16[512,4,128]{0,2,1:T(8,128)(2,1)S(1)} %fusion.28) | copy-start | bytes 1572868
  382.4 5.1 copy-start.24
  382.4 150.1 %reduce-scatter.5.cloned.1.call-start = ((), (), s32[]{:S(2)}) async-start(), calls=%async_computation.5 | async-start | bytes 5242880 | tf_op jit(solution)/shard_map/reduce_scatter | solution.py:215
  382.7 4.8 copy-start.21
  387.5 5.9 %copy-start.8 = (bf16[32,128,512]{2,1,0:T(8,128)(2,1)S(1)}, bf16[32,128,512]{2,1,0:T(8,128)(2,1)}, u32[]{:S(2)}) copy-start(bf16[32,128,512]{2,1,0:T(8,128)(2,1)} %copy-done.7) | copy-start | bytes 12582916
Sparse Core Ops, SparseCore 0:
  10.2 72.0 all-gather.12
  84.6 45.1 all-gather.10
  132.6 52.1 all-gather.14
  192.9 110.4 all-gather.16
  382.5 99.3 reduce-scatter.6
  484.8 47.7 reduce-scatter.4
